TPU v7x, 32 devices: a whole 2x2x4 slice. The times are simulated.
32 devices in a mesh: ids: 8 (over z, x), mdl: 4 (over y, core).
Axes of the slice: x: 2, y: 2, z: 4, core: 2. Of those that a mesh axis runs over, the one named last changes fastest.
Arguments:
- hash_codes: int32 [32768, 1024], P('ids', 'mdl'), may hold values from 0 to 1023
- request_ids: int32 [64, 1024], P('ids'), may hold values from 0 to 32767, as said below
- request_counts: int32 [64], P('ids'), may hold values from 256 to 1024, as said below
- token_slots: int32 [65536], P('ids'), may hold values from 0 to 8191, as said below
- cotangent: bfloat16 [65536, 32], P('ids'), may hold values from -6 to 6
- weight_first: float32 [1024, 1800], P('ids', 'mdl'), may hold values from -0.1875 to 0.1875
- weight_second: float32 [1800, 1800], P(None, 'mdl'), may hold values from -0.125 to 0.125
- weight_final: float32 [1800, 32], P('mdl'), may hold values from -0.125 to 0.125
- norm_params: float32 [4, 1800], P(None, 'mdl')
- bias_final: float32 [32], replicated, may hold values from -0.5 to 0.5
- moment_first: float32 [1024, 1800], P('ids', 'mdl'), may hold values from -0.0007324219 to 0.0007324219
- square_first: float32 [1024, 1800], P('ids', 'mdl'), may hold values from 1.373291e-09 to 5.493164e-09
- moment_second: float32 [1800, 1800], P(None, 'mdl'), may hold values from -0.0007324219 to 0.0007324219
- square_second: float32 [1800, 1800], P(None, 'mdl'), may hold values from 1.373291e-09 to 5.493164e-09
- moment_final: float32 [1800, 32], P('mdl'), may hold values from -0.0048828125 to 0.0048828125
- square_final: float32 [1800, 32], P('mdl'), may hold values from 6.103516e-08 to 2.4414064e-07
- moment_norm: float32 [4, 1800], P(None, 'mdl'), may hold values from -0.001953125 to 0.001953125
- square_norm: float32 [4, 1800], P(None, 'mdl'), may hold values from 9e-09 to 3.6e-08
- moment_bias: float32 [32], replicated, may hold values from -0.03125 to 0.03125
- square_bias: float32 [32], replicated, may hold values from 2.5e-06 to 1e-05
Outputs:
- token_embed: bfloat16 [65536, 32], P('ids')
- momentum_first: float32 [1024, 1800], P('ids', 'mdl')
- variance_first: float32 [1024, 1800], P('ids', 'mdl')
- master_first: float32 [1024, 1800], P('ids', 'mdl')
- bfloat_first: bfloat16 [1024, 1800], P('ids', 'mdl')
- momentum_second: float32 [1800, 1800], P(None, 'mdl')
- variance_second: float32 [1800, 1800], P(None, 'mdl')
- master_second: float32 [1800, 1800], P(None, 'mdl')
- bfloat_second: bfloat16 [1800, 1800], P(None, 'mdl')
- momentum_final: float32 [1800, 32], P('mdl')
- variance_final: float32 [1800, 32], P('mdl')
- master_final: float32 [1800, 32], P('mdl')
- bfloat_final: bfloat16 [1800, 32], P('mdl')
- momentum_norm: float32 [4, 1800], P(None, 'mdl')
- variance_norm: float32 [4, 1800], P(None, 'mdl')
- master_norm: float32 [4, 1800], P(None, 'mdl')
- momentum_bias: float32 [32], replicated
- variance_bias: float32 [32], replicated
- master_bias: float32 [32], replicated
Inputs may be any that keep to these rules, and one draw needn't show every extreme that they name: `request_ids`: entries of row s * 8 + j lie in owner j's range j * 4096 to (j + 1) * 4096 - 1; the live ones (the first request_counts of the row) are distinct; the others are padding. `request_counts`: some owner receives exactly 1024 live ids from every device. `token_slots`: each token points at a live slot of its own device, and every live slot of a device is pointed at by one or more of its tokens.
All inputs are finite; a program needn't handle non-finite values.
Results may differ from a plain program's by a relative error of at most 0.003.
The roundings to bfloat16 on the way count: a program that leaves them out, or rounds other values in their place, can miss the bound.
Values may be sent and summed in bfloat16 or wider, within the bound.
A program may use at most 256 MiB of HBM per device.

v0:
```python
import jax
import jax.numpy as jnp
from jax import lax
from jax.sharding import PartitionSpec as P

STEP = 10
beta_one = 0.9
beta_two = 0.999
adam_epsilon = 1e-08
norm_epsilon = 1e-05
penalty_weight = 0.25
decay_matrix = 0.01
rate_matrix = 0.05
rate_norm = 0.5
rate_bias = 0.02
LANES = 128


def mish_parts(inputs):
    grown = jnp.exp(jnp.minimum(inputs, 20.0))
    above = grown * (grown + 2.0)
    inverse = 1.0 / (above + 2.0)
    return (grown, above * inverse, inverse)


def mish(inputs):
    return inputs * mish_parts(inputs)[1]


def mish_slope(inputs):
    grown, gate, inverse = mish_parts(inputs)
    return gate + 4.0 * jnp.minimum(inputs, 20.0) * (grown * inverse) * ((1.0 + grown) * inverse)


def contract(left, right, left_dim, right_dim):
    return lax.dot_general(
        left, right, (((left_dim,), (right_dim,)), ((), ())), preferred_element_type=jnp.float32
    )


def norm_back(upstream, unit_rows, gain_row, scale_row, live_mask, gain_sum, shift_sum, live_count):
    return scale_row * (
        gain_row * upstream
        - live_mask[:, None] * gain_row * (shift_sum + unit_rows * gain_sum) / live_count
    )


def adam(weight, moment, square, gradient, step_rate, shrink):
    momentum = beta_one * moment + (1.0 - beta_one) * gradient
    variance = beta_two * square + (1.0 - beta_two) * gradient * gradient
    moment_hat = momentum / (1.0 - beta_one**STEP)
    square_hat = variance / (1.0 - beta_two**STEP)
    master = weight - step_rate * (
        moment_hat / (jnp.sqrt(square_hat) + adam_epsilon) + shrink * weight
    )
    return (momentum, variance, master)


def split_two(values):
    high = values.astype(jnp.bfloat16)
    low = (values - high.astype(jnp.float32)).astype(jnp.bfloat16)
    return (high, low)


def one_hot(index, length, first):
    rows = lax.broadcasted_iota(jnp.int32, (length, index.shape[0]), 0) + first
    return (rows == index[None, :]).astype(jnp.bfloat16)


def body(
    hash_codes,
    request_ids,
    request_counts,
    token_slots,
    cotangent,
    weight_first,
    weight_second,
    weight_final,
    norm_params,
    bias_final,
    moment_first,
    square_first,
    moment_second,
    square_second,
    moment_final,
    square_final,
    moment_norm,
    square_norm,
    moment_bias,
    square_bias,
):
    owners = lax.axis_size("ids")
    parts = lax.axis_size("mdl")
    part = lax.axis_index("mdl")
    both = ("ids", "mdl")
    range_rows = hash_codes.shape[0]
    rows = range_rows // parts
    slots_per = request_ids.shape[1]
    piece = slots_per // parts
    out_width = weight_final.shape[1]
    width = weight_first.shape[1]
    wide = width + -width % LANES
    hidden = wide * parts
    more = wide - width
    token_count = token_slots.shape[0]
    token_piece = token_count // parts
    token_total = token_count * owners
    first_part = jnp.pad(weight_first.astype(jnp.bfloat16), ((0, 0), (0, more)))
    first_low = lax.all_gather(first_part, "ids", axis=0, tiled=True)
    first_low = lax.all_gather(first_low, "mdl", axis=1, tiled=True)
    second_part = jnp.pad(
        weight_second.astype(jnp.bfloat16).reshape(parts, width, width),
        ((0, 0), (0, more), (0, more)),
    ).reshape(hidden, wide)
    second_low = lax.all_gather(second_part, "mdl", axis=1, tiled=True)
    final_part = jnp.pad(weight_final.astype(jnp.bfloat16), ((0, more), (0, 0)))
    final_low = lax.all_gather(final_part, "mdl", axis=0, tiled=True)
    norm_all = lax.all_gather(jnp.pad(norm_params, ((0, 0), (0, more))), "mdl", axis=1, tiled=True)
    encoded = ((hash_codes.astype(jnp.float32) + 0.5) / 512.0 - 1.0).astype(jnp.bfloat16)
    features = lax.all_to_all(encoded, "mdl", split_axis=0, concat_axis=1, tiled=True)
    owner_row = jnp.arange(owners, dtype=jnp.int32)[:, None]
    wanted = jnp.where(
        jnp.arange(slots_per, dtype=jnp.int32)[None, :] < request_counts[:, None],
        request_ids - owner_row * range_rows,
        range_rows,
    )
    received = lax.all_to_all(wanted, "ids", split_axis=0, concat_axis=0, tiled=True)
    slot_owner = token_slots // slots_per
    slot_place = token_slots % slots_per - part * piece
    slot_here = jnp.where(
        (slot_place >= 0) & (slot_place < piece), slot_owner * piece + slot_place, -1
    )
    slot_sum = (
        jnp.dot(
            one_hot(slot_here, owners * piece, 0), cotangent, preferred_element_type=jnp.float32
        )
        / token_total
    )
    high, low = split_two(slot_sum)
    sent = jnp.concatenate([high, low], axis=1).reshape(owners, piece * 2 * out_width)
    arrived = lax.all_to_all(sent, "ids", split_axis=0, concat_axis=0, tiled=True)
    arrived = lax.all_gather(
        arrived.reshape(owners * piece, 2 * out_width), "mdl", axis=0, tiled=False
    )
    arrived = arrived.reshape(parts * owners * piece, 2 * out_width)
    slot_rows = received.reshape(owners, parts, piece).transpose(1, 0, 2)
    slot_rows = slot_rows.reshape(-1)
    marked = jnp.concatenate(
        [arrived, jnp.ones((arrived.shape[0], 2 * out_width), jnp.bfloat16)], axis=1
    )
    row_sums = jnp.dot(
        one_hot(slot_rows, rows, part * rows), marked, preferred_element_type=jnp.float32
    )
    row_grad = row_sums[:, :out_width] + row_sums[:, out_width : 2 * out_width]
    live_mask = jnp.minimum(row_sums[:, 2 * out_width], 1.0)
    linear_one = jnp.dot(features, first_low, preferred_element_type=jnp.float32)
    active_one = mish(linear_one)
    weighted_one = live_mask[:, None] * active_one
    sums_one = jnp.stack([jnp.sum(weighted_one, 0), jnp.sum(weighted_one * active_one, 0)])
    sums_one, live_count = lax.psum((sums_one, jnp.sum(live_mask)), both)
    mean_one = sums_one[0] / live_count
    scale_one = lax.rsqrt(sums_one[1] / live_count - mean_one * mean_one + norm_epsilon)
    unit_one = (active_one - mean_one) * scale_one
    normed_one = (norm_all[0] * unit_one + norm_all[1]).astype(jnp.bfloat16)
    linear_two = jnp.dot(normed_one, second_low, preferred_element_type=jnp.float32)
    active_two = mish(linear_two)
    weighted_two = live_mask[:, None] * active_two
    sums_two = lax.psum(
        jnp.stack([jnp.sum(weighted_two, 0), jnp.sum(weighted_two * active_two, 0)]), both
    )
    mean_two = sums_two[0] / live_count
    scale_two = lax.rsqrt(sums_two[1] / live_count - mean_two * mean_two + norm_epsilon)
    unit_two = (active_two - mean_two) * scale_two
    normed_two = (norm_all[2] * unit_two + norm_all[3]).astype(jnp.bfloat16)
    embedding = jnp.dot(normed_two, final_low, preferred_element_type=jnp.float32) + bias_final
    embed_low = embedding.astype(jnp.bfloat16)
    embed_range = lax.all_gather(embed_low, "mdl", axis=0, tiled=True)
    slots_mine = lax.dynamic_slice(received, (0, part * piece), (owners, piece)).reshape(-1)
    pick_rows = (
        slots_mine[:, None] == lax.broadcasted_iota(jnp.int32, (owners * piece, range_rows), 1)
    ).astype(jnp.bfloat16)
    replies = jnp.dot(pick_rows, embed_range, preferred_element_type=jnp.float32)
    replies = replies.astype(jnp.bfloat16).reshape(owners, piece * out_width)
    returned = lax.all_to_all(replies, "ids", split_axis=0, concat_axis=0, tiled=True)
    returned = lax.all_gather(returned.reshape(owners, piece, out_width), "mdl", axis=1, tiled=True)
    returned = returned.reshape(owners * slots_per, out_width)
    tokens_mine = lax.dynamic_slice(token_slots, (part * token_piece,), (token_piece,))
    pick_slots = (
        tokens_mine[:, None]
        == lax.broadcasted_iota(jnp.int32, (token_piece, owners * slots_per), 1)
    ).astype(jnp.bfloat16)
    token_part = jnp.dot(pick_slots, returned, preferred_element_type=jnp.float32)
    token_embed = lax.all_gather(token_part.astype(jnp.bfloat16), "mdl", axis=0, tiled=True)
    grad_embed = (
        row_grad + 2.0 * penalty_weight / live_count * live_mask[:, None] * embedding
    ).astype(jnp.bfloat16)
    incoming_two = contract(grad_embed, final_low, 1, 1)
    sums_two = lax.psum(
        jnp.stack([jnp.sum(incoming_two * unit_two, 0), jnp.sum(incoming_two, 0)]), both
    )
    local_final = contract(normed_two, grad_embed, 0, 0)
    local_bias = jnp.sum(grad_embed.astype(jnp.float32), 0)
    outgoing_two = norm_back(
        incoming_two,
        unit_two,
        norm_all[2],
        scale_two,
        live_mask,
        sums_two[0],
        sums_two[1],
        live_count,
    )
    grad_linear_two = (mish_slope(linear_two) * outgoing_two).astype(jnp.bfloat16)
    local_second = jnp.stack(
        [
            contract(normed_one, grad_linear_two[:, wide * k : wide * (k + 1)], 0, 0)
            for k in range(parts)
        ]
    )
    grad_second = lax.psum_scatter(local_second, "mdl", scatter_dimension=0, tiled=False)
    grad_second = lax.psum(grad_second, "ids")
    grad_second = grad_second.reshape(parts, wide, wide)[:, :width, :width].reshape(-1, width)
    incoming_one = contract(grad_linear_two, second_low, 1, 1)
    sums_one, final_sum, grad_bias = lax.psum(
        (
            jnp.stack([jnp.sum(incoming_one * unit_one, 0), jnp.sum(incoming_one, 0)]),
            local_final,
            local_bias,
        ),
        both,
    )
    outgoing_one = norm_back(
        incoming_one,
        unit_one,
        norm_all[0],
        scale_one,
        live_mask,
        sums_one[0],
        sums_one[1],
        live_count,
    )
    grad_linear_one = (mish_slope(linear_one) * outgoing_one).astype(jnp.bfloat16)
    local_first = jnp.stack(
        [
            contract(features, grad_linear_one[:, wide * k : wide * (k + 1)], 0, 0)
            for k in range(parts)
        ]
    )
    grad_first = lax.psum_scatter(local_first, "mdl", scatter_dimension=0, tiled=False)
    grad_first = lax.psum_scatter(grad_first, "ids", scatter_dimension=0, tiled=True)[:, :width]
    start = part * wide
    grad_final = lax.dynamic_slice(final_sum, (start, 0), (width, out_width))
    grad_norm = lax.dynamic_slice(jnp.concatenate([sums_one, sums_two]), (0, start), (4, width))
    momentum_first, variance_first, master_first = adam(
        weight_first, moment_first, square_first, grad_first, rate_matrix, decay_matrix
    )
    momentum_second, variance_second, master_second = adam(
        weight_second, moment_second, square_second, grad_second, rate_matrix, decay_matrix
    )
    momentum_final, variance_final, master_final = adam(
        weight_final, moment_final, square_final, grad_final, rate_matrix, decay_matrix
    )
    momentum_norm, variance_norm, master_norm = adam(
        norm_params, moment_norm, square_norm, grad_norm, rate_norm, 0.0
    )
    momentum_bias, variance_bias, master_bias = adam(
        bias_final, moment_bias, square_bias, grad_bias, rate_bias, 0.0
    )
    return (
        token_embed,
        momentum_first,
        variance_first,
        master_first,
        master_first.astype(jnp.bfloat16),
        momentum_second,
        variance_second,
        master_second,
        master_second.astype(jnp.bfloat16),
        momentum_final,
        variance_final,
        master_final,
        master_final.astype(jnp.bfloat16),
        momentum_norm,
        variance_norm,
        master_norm,
        momentum_bias,
        variance_bias,
        master_bias,
    )


def solution(mesh):
    rows = P("ids", None)
    grid = P("ids", "mdl")
    columns = P(None, "mdl")
    mdl_rows = P("mdl", None)
    return jax.shard_map(
        body,
        mesh=mesh,
        in_specs=(grid, rows, P("ids"), P("ids"), rows, grid, columns, mdl_rows, columns, P())
        + (grid,) * 2
        + (columns,) * 2
        + (mdl_rows,) * 2
        + (columns,) * 2
        + (P(),) * 2,
        out_specs=(rows,)
        + (grid,) * 4
        + (columns,) * 4
        + (mdl_rows,) * 4
        + (columns,) * 3
        + (P(),) * 3,
        check_vma=False,
    )
```

profile of v0, /device:TPU:0, one launch (start us, length us, event | category | flops | bytes accessed | tf_op | source)
XLA Modules:
  0.0 1000.3 jit_solution(2400045335157976259)
XLA Ops:
  9.8 13.0 %subtract_convert_fusion = (bf16[2048,32]{0,1:T(8,128)(2,1)S(1)}, bf16[2048,32]{0,1:T(8,128)(2,1)S(1)}) fusion(bf16[8192,32]{0,1:T(8,128)(2,1)S(1)} %copy-done, s32[8192]{0:T(1024)S(1)} %fusion.37), kind=kOutput, calls=%fused_computation.68 | convolution fusion | flops 1090846720 | bytes 819200 | tf_op jit(solution)/shard_map/dot_general | solution.py:134
  26.4 18.5 %all_to_all.48 = bf16[8,2,8192]{2,1,0:T(2,128)(2,1)S(1)} all-to-all(bf16[8,2,8192]{2,1,0:T(2,128)(2,1)S(1)} %reshape.107), channel_id=1, replica_groups=mesh['ids'=8,'mdl'=4] {'ids'}, dimensions={0} | all-to-all | bytes 524288 | tf_op jit(solution)/shard_map/all_to_all | solution.py:141
  81.7 48.9 %all_gather.27 = f32[4,2048]{1,0:T(4,128)S(1)} all-gather(f32[4,512]{1,0:T(4,128)S(1)} %pad.17), channel_id=1, replica_groups=mesh['ids'=8,'mdl'=4] {'mdl'}, dimensions={1}, use_global_device_ids=true | all-gather | bytes 40960 | tf_op jit(solution)/shard_map/all_gather | solution.py:118
  147.0 11.5 %multiply_reduce_fusion.1 = (f32[2048]{0:T(1024)S(1)}, f32[2048]{0:T(1024)S(1)}, f32[1024,2048]{1,0:T(8,128)}) fusion(f32[1024]{0:T(1024)S(1)} %bitcast.109, bf16[1024,1024]{0,1:T(8,128)(2,1)S(1)} %bitcast.85, bf16[1024,2048]{0,1:T(8,128)(2,1)} %all-gather.7.cloned.1.call-done), kind=kOutput, calls=%fused_computation.19 | convolution fusion | flops 4318031872 | bytes 14700544 | tf_op jit(solution)/shard_map/dot_general | solution.py:156
  158.5 39.1 %all-reduce.6 = (f32[2,2048]{1,0:T(2,128)S(1)}, f32[]{:T(128)}) all-reduce(f32[2,2048]{1,0:T(2,128)S(1)} %pad_maximum_fusion.3, f32[]{:T(128)} %get-tuple-element.151), channel_id=1, replica_groups=mesh['ids'=8,'mdl'=4] {'ids','mdl'}, use_global_device_ids=true, to_apply=%region_2.3 | all-reduce | flops 4097 | bytes 32776 | tf_op jit(solution)/shard_map/psum | solution.py:160
  198.9 7.3 add_convert_fusion.1
  206.2 18.3 %multiply_reduce_fusion = (f32[2048]{0:T(1024)S(1)}, f32[2048]{0:T(1024)S(1)}, f32[1024,2048]{1,0:T(8,128)}, f32[1024,2048]{1,0:T(8,128)}) fusion(f32[1024]{0:T(1024)S(1)} %bitcast.110, bf16[1024,2048]{1,0:T(8,128)(2,1)} %add_convert_fusion.1, bf16[2048,2048]{0,1:T(8,128)(2,1)} %all-gather.11.cloned.1.call-done), kind=kOutput, calls=%fused_computation.17 | convolution fusion | flops 8612999168 | bytes 29380608 | tf_op jit(solution)/shard_map/dot_general | solution.py:165
  224.5 40.1 %psum.58 = f32[2,2048]{1,0:T(2,128)S(1)} all-reduce(f32[2,2048]{1,0:T(2,128)S(1)} %pad_maximum_fusion.4), channel_id=1, replica_groups=mesh['ids'=8,'mdl'=4] {'ids','mdl'}, use_global_device_ids=true, to_apply=%region_7.8 | all-reduce | flops 4096 | bytes 32768 | tf_op jit(solution)/shard_map/psum | solution.py:168
  274.9 40.2 %psum.59 = f32[2,2048]{1,0:T(2,128)S(1)} all-reduce(f32[2,2048]{1,0:T(2,128)S(1)} %pad_maximum_fusion.5), channel_id=1, replica_groups=mesh['ids'=8,'mdl'=4] {'ids','mdl'}, use_global_device_ids=true, to_apply=%region_10.11 | all-reduce | flops 4096 | bytes 32768 | tf_op jit(solution)/shard_map/psum | solution.py:198
  315.1 12.7 %multiply_convert_fusion.1 = bf16[1024,2048]{1,0:T(8,128)(2,1)S(1)} fusion(f32[1024,2048]{1,0:T(8,128)} %get-tuple-element.167, f32[1024,2048]{1,0:T(8,128)} %get-tuple-element.165, f32[1024,2048]{1,0:T(8,128)} %get-tuple-element.148, f32[]{:T(128)} %get-tuple-element.125, f32[2048]{0:T(1024)S(1)} %bitcast.120, f32[2048]{0:T(1024)S(1)} %bitcast.119, ...), kind=kLoop, calls=%fused_computation.25 | loop fusion | flops 52428800 | bytes 29405188 | tf_op jit(solution)/shard_map/convert_element_type | solution.py:213
  327.8 18.4 %multiply_reduce_fusion.2 = (f32[2048]{0:T(1024)S(1)}, f32[2048]{0:T(1024)S(1)}, f32[1024,2048]{1,0:T(8,128)}) fusion(f32[2048]{0:T(1024)S(1)} %bitcast.94, f32[2048]{0:T(1024)S(1)} %bitcast.97, f32[1024,2048]{1,0:T(8,128)} %get-tuple-element.164, bf16[1024,2048]{1,0:T(8,128)(2,1)S(1)} %multiply_convert_fusion.1, ...), kind=kOutput, calls=%fused_computation.24 | convolution fusion | flops 8615096320 | bytes 29392896 | tf_op jit(solution)/shard_map/dot_general | solution.py:36
  346.2 40.7 %all-reduce.5 = (f32[2,2048]{1,0:T(2,128)S(1)}, f32[32]{0:T(128)S(1)}) all-reduce(f32[2,2048]{1,0:T(2,128)S(1)} %pad_maximum_fusion.6, f32[32]{0:T(128)S(1)} %get-tuple-element.144), channel_id=1, replica_groups=mesh['ids'=8,'mdl'=4] {'ids','mdl'}, use_global_device_ids=true, to_apply=%region_13.14 | all-reduce | flops 4128 | bytes 33024 | tf_op jit(solution)/shard_map/psum | solution.py:224
  386.9 11.3 %multiply_convert_fusion = bf16[1024,2048]{1,0:T(8,128)(2,1)S(1)} fusion(f32[1024,2048]{1,0:T(8,128)} %get-tuple-element.168, f32[1024,2048]{1,0:T(8,128)} %get-tuple-element.164, f32[2048]{0:T(1024)S(1)} %bitcast.114, f32[2048]{0:T(1024)S(1)} %bitcast.113, f32[]{:T(128)} %get-tuple-element.125, f32[2048]{0:T(1024)S(1)} %bitcast.95, f32[2048]{0:T(1024)S(1)} %bitcast.98, ...), kind=kLoop, calls=%fused_computation.23 | loop fusion | flops 54525952 | bytes 21016580 | tf_op jit(solution)/shard_map/convert_element_type | solution.py:242
  419.4 6.5 pad_maximum_fusion
  431.8 47.1 %reduce-scatter.4.cloned.1.call-done = f32[1,1024,512]{2,1,0:T(8,128)} async-done(((f32[4,1024,512]{2,1,0:T(8,128)}), f32[1,1024,512]{2,1,0:T(8,128)}) %reduce-scatter.4.cloned.1.call-update) | async-done | bytes 2097168 | tf_op jit(solution)/shard_map/reduce_scatter | solution.py:249
  479.0 127.4 %reduce-scatter.8.cloned.1.call-done = f32[1,2048,512]{2,1,0:T(8,128)} async-done(((f32[4,2048,512]{2,1,0:T(8,128)}), f32[1,2048,512]{2,1,0:T(8,128)}) %reduce-scatter.8.cloned.1.call-update) | async-done | bytes 4194320 | tf_op jit(solution)/shard_map/reduce_scatter | solution.py:220
  613.7 6.8 fusion.18
  630.0 109.6 %all-reduce.12.cloned.1.call-done = f32[2048,32]{0,1:T(8,128)} async-done(((f32[2048,32]{0,1:T(8,128)}), f32[2048,32]{0,1:T(8,128)}) %all-reduce.12.cloned.1.call-update) | async-done | bytes 262160 | tf_op jit(solution)/shard_map/psum | solution.py:224
  742.6 15.7 %all_gather.34 = bf16[8,1024,32]{2,1,0:T(8,128)(2,1)S(1)} all-gather(bf16[8,256,32]{2,1,0:T(8,128)(2,1)S(1)} %reshape.98), channel_id=1, replica_groups=mesh['ids'=8,'mdl'=4] {'mdl'}, dimensions={1}, use_global_device_ids=true | all-gather | bytes 655360 | tf_op jit(solution)/shard_map/all_gather | solution.py:185
  758.3 14.1 %fusion.19 = bf16[2048,32]{0,1:T(8,128)(2,1)S(1)} fusion(bf16[8192,32]{1,0:T(8,128)(2,1)S(1)} %bitcast.83, s32[2048]{0:T(1024)S(1)} %dynamic-slice-done), kind=kOutput, calls=%fused_computation.48 | convolution fusion | flops 1090584576 | bytes 663552 | tf_op jit(solution)/shard_map/dot_general | solution.py:192
  772.4 7.5 all_gather.35
  779.9 30.7 %reduce-scatter.6.cloned.1.call-done = f32[128,512]{1,0:T(8,128)} async-done(((f32[1024,512]{1,0:T(8,128)}), f32[128,512]{1,0:T(8,128)}) %reduce-scatter.6.cloned.1.call-update) | async-done | bytes 262160 | tf_op jit(solution)/shard_map/reduce_scatter | solution.py:250
  815.0 154.8 %all-reduce.10.cloned.1.call-done = f32[4,512,512]{2,1,0:T(8,128)} async-done(((f32[4,512,512]{2,1,0:T(8,128)}), f32[4,512,512]{2,1,0:T(8,128)}) %all-reduce.10.cloned.1.call-update) | async-done | bytes 4194320 | tf_op jit(solution)/shard_map/psum | solution.py:221
  983.5 9.0 fusion.48
  (156 shorter events, 135.5 us)
Async XLA Ops:
  7.2 46.1 %all-gather.5.cloned.1.call-start = ((), (), s32[]{:S(2)}) async-start(), calls=%async_computation.7 | async-start | bytes 1179648 | tf_op jit(solution)/shard_map/all_gather | solution.py:109
  9.0 129.6 %all-gather.9.cloned.1.call-start = ((), (), s32[]{:S(2)}) async-start(), calls=%async_computation.9 | async-start | bytes 1310720 | tf_op jit(solution)/shard_map/all_gather | solution.py:142
  48.2 98.8 %all-gather.7.cloned.1.call-start = ((), (), s32[]{:S(2)}) async-start(), calls=%async_computation.8 | async-start | bytes 5242880 | tf_op jit(solution)/shard_map/all_gather | solution.py:110
  53.3 152.9 %all-gather.11.cloned.1.call-start = ((), (), s32[]{:S(2)}) async-start(), calls=%async_computation.10 | async-start | bytes 10485760 | tf_op jit(solution)/shard_map/all_gather | solution.py:115
  66.3 11.7 %all-to-all-start = ((s32[8,1,1024]{2,1,0:T(1,128)}), s32[8,1,1024]{2,1,0:T(1,128)S(1)}, u32[]{:S(2)}, u32[]{:S(2)}) async-start(s32[8,1,1024]{2,1,0:T(1,128)} %all_to_all.32), calls=%async_computation | async-start | bytes 65536 | tf_op jit(solution)/shard_map/all_to_all | solution.py:127
  78.0 68.4 %copy-start.12 = (s32[8,1,1024]{2,1,0:T(1,128)}, s32[8,1,1024]{2,1,0:T(1,128)S(1)}, u32[]{:S(2)}) copy-start(s32[8,1,1024]{2,1,0:T(1,128)S(1)} %all-to-all-done) | copy-start | bytes 98308
  78.0 58.2 %all-to-all-start.1 = ((bf16[4,1024,256]{2,1,0:T(8,128)(2,1)}), bf16[4,1024,256]{2,1,0:T(8,128)(2,1)S(1)}, u32[]{:S(2)}, u32[]{:S(2)}) async-start(bf16[4,1024,256]{2,1,0:T(8,128)(2,1)} %bitcast.3), calls=%async_computation.1 | async-start | bytes 4194304 | tf_op jit(solution)/shard_map/all_to_all | solution.py:120
  81.6 397.3 %reduce-scatter.4.cloned.1.call-start = ((), (), s32[]{:S(2)}) async-start(), calls=%async_computation.11 | async-start | bytes 10485760 | tf_op jit(solution)/shard_map/reduce_scatter | solution.py:249
  206.2 59.3 %copy-start.21 = (f32[32]{0:T(128)S(1)}, f32[32]{0:T(128)}, u32[]{:S(2)}) copy-start(f32[32]{0:T(128)} %param.29) | copy-start | bytes 388
  406.9 199.5 %reduce-scatter.8.cloned.1.call-start = ((), (), s32[]{:S(2)}) async-start(), calls=%async_computation.13 | async-start | bytes 20971520 | tf_op jit(solution)/shard_map/reduce_scatter | solution.py:220
  426.0 180.5 %copy-start.7 = (f32[128,450]{0,1:T(8,128)S(1)}, f32[128,450]{0,1:T(8,128)}, u32[]{:S(2)}) copy-start(f32[128,450]{0,1:T(8,128)} %param.25) | copy-start | bytes 691204
  426.0 180.7 %copy-start.10 = (f32[128,450]{0,1:T(8,128)S(1)}, f32[128,450]{0,1:T(8,128)}, u32[]{:S(2)}) copy-start(f32[128,450]{0,1:T(8,128)} %param.31) | copy-start | bytes 691204
  426.0 180.8 %copy-start.11 = (f32[128,450]{0,1:T(8,128)S(1)}, f32[128,450]{0,1:T(8,128)}, u32[]{:S(2)}) copy-start(f32[128,450]{0,1:T(8,128)} %param.30) | copy-start | bytes 691204
  426.0 313.6 %all-reduce.12.cloned.1.call-start = ((), (), s32[]{:S(2)}) async-start(), calls=%async_computation.15 | async-start | bytes 524288 | tf_op jit(solution)/shard_map/psum | solution.py:224
  431.8 378.8 %reduce-scatter.6.cloned.1.call-start = ((), (), s32[]{:S(2)}) async-start(), calls=%async_computation.12 | async-start | bytes 2359296 | tf_op jit(solution)/shard_map/reduce_scatter | solution.py:250
  478.9 490.8 %all-reduce.10.cloned.1.call-start = ((), (), s32[]{:S(2)}) async-start(), calls=%async_computation.14 | async-start | bytes 8388608 | tf_op jit(solution)/shard_map/psum | solution.py:221
  606.6 22.7 %copy-start.16 = (f32[4,450]{1,0:T(4,128)S(1)}, f32[4,450]{1,0:T(4,128)}, u32[]{:S(2)}) copy-start(f32[4,450]{1,0:T(4,128)} %param.28) | copy-start | bytes 21604
  606.6 22.7 %copy-start.18 = (f32[4,450]{1,0:T(4,128)S(1)}, f32[4,450]{1,0:T(4,128)}, u32[]{:S(2)}) copy-start(f32[4,450]{1,0:T(4,128)} %param.37) | copy-start | bytes 21604
  606.6 22.7 %copy-start.19 = (f32[4,450]{1,0:T(4,128)S(1)}, f32[4,450]{1,0:T(4,128)}, u32[]{:S(2)}) copy-start(f32[4,450]{1,0:T(4,128)} %param.36) | copy-start | bytes 21604
  606.7 133.0 %copy-start.9 = (f32[450,32]{0,1:T(8,128)S(1)}, f32[450,32]{0,1:T(8,128)}, u32[]{:S(2)}) copy-start(f32[450,32]{0,1:T(8,128)} %param.27) | copy-start | bytes 172804
  606.7 133.0 %copy-start.13 = (f32[450,32]{0,1:T(8,128)S(1)}, f32[450,32]{0,1:T(8,128)}, u32[]{:S(2)}) copy-start(f32[450,32]{0,1:T(8,128)} %param.35) | copy-start | bytes 172804
  606.7 133.0 %copy-start.14 = (f32[450,32]{0,1:T(8,128)S(1)}, f32[450,32]{0,1:T(8,128)}, u32[]{:S(2)}) copy-start(f32[450,32]{0,1:T(8,128)} %param.34) | copy-start | bytes 172804
  613.7 144.6 %dynamic-slice-start = ((s32[8192]{0:T(1024)}, s32[]{:T(128)}), s32[2048]{0:T(1024)S(1)}, s32[]{:S(2)}) async-start(s32[8192]{0:T(1024)} %param.23, s32[]{:T(128)} %select_n.30), calls=%async_computation.16 | async-start | bytes 16896 | tf_op jit(solution)/shard_map/dynamic_slice | solution.py:187
  623.3 118.1 %all-to-all-start.3 = ((bf16[8,2,4096]{2,1,0:T(2,128)(2,1)}), bf16[8,2,4096]{2,1,0:T(2,128)(2,1)S(1)}, u32[]{:S(2)}, u32[]{:S(2)}) async-start(bf16[8,2,4096]{2,1,0:T(2,128)(2,1)} %reshape.109), calls=%async_computation.3 | async-start | bytes 262144 | tf_op jit(solution)/shard_map/all_to_all | solution.py:184
  (13 other events, 164.2 us)
Sparse Core Ops, SparseCore 0:
  10.6 42.5 all-gather.4
  55.4 17.2 all-gather.8
  74.3 56.9 all-gather.6
  133.3 57.1 all-gather.10
  407.0 71.8 reduce-scatter.3
  481.3 125.0 reduce-scatter.7
  612.5 127.0 all-reduce.11
  743.2 67.4 reduce-scatter.5
  814.3 155.4 all-reduce.9
where the time goes:
time: 1010 us; the launch traced here: 1000 us
  waiting for transfers between devices  477 us (47%)
  blocking collectives  262 us (26%)
  matrix products  121 us (12%)
  other arithmetic  72.2 us (7%)
  local copies, waits for them, and re-layouts  37.4 us (4%)
  between operations  15.7 us (2%)
  starting transfers between devices  15 us (1%)
    psum x1, waiting for transfers between devices, body(): grad_second = lax.psum(grad_second, 'ids')  155 us
    reduce_scatter x1, waiting for transfers between devices, body(): lax.psum_scatter(local_second, 'mdl', scatter_dimension=0, tiled=False)  127 us
    psum x1, waiting for transfers between devices, body(): lax.psum((jnp.stack([jnp.sum(incoming_one * unit_one, 0), jnp.sum(incomin...  110 us
    all_gather x1, blocking collectives, body(): lax.all_gather(jnp.pad(norm_params, ((0, 0), (0, more))), 'mdl', axis=1,...  48.9 us
    reduce_scatter x1, waiting for transfers between devices, body(): lax.psum_scatter(local_first, 'mdl', scatter_dimension=0, tiled=False)  47.1 us
    dot_general x11, matrix products, contract(): lax.dot_general(left, right, (((left_dim,), (right_dim,)), ((), ())), pre...  45.5 us
    psum x1, blocking collectives, body(): lax.psum((jnp.stack([jnp.sum(incoming_one * unit_one, 0), jnp.sum(incomin...  40.7 us
    psum x1, blocking collectives, body(): lax.psum(jnp.stack([jnp.sum(incoming_two * unit_two, 0), jnp.sum(incoming...  40.2 us
  transfers between devices with their start and end apart: 12, of which 7 were waited for; matrix products, arithmetic and copies ran while one was open for 12% of the time, Pallas kernels for 0%

commit v1 on v0

--- a/solution.py
+++ b/solution.py
@@ -218,7 +218,7 @@
         ]
     )
     grad_second = lax.psum_scatter(local_second, "mdl", scatter_dimension=0, tiled=False)
-    grad_second = lax.psum(grad_second, "ids")
+    grad_second = jnp.sum(lax.all_gather(grad_second, "ids"), axis=0)
     grad_second = grad_second.reshape(parts, wide, wide)[:, :width, :width].reshape(-1, width)
     incoming_one = contract(grad_linear_two, second_low, 1, 1)
     sums_one, final_sum, grad_bias = lax.psum(

time: 1010 us -> 1500 us (1.49)
  waiting for transfers between devices: 477 us -> 956 us
  other arithmetic: 72.2 us -> 87.3 us
    all_gather x0 -> x1, waiting for transfers between devices: none -> 634 us  [body(): grad_second = jnp.sum(lax.all_gather(grad_second, 'ids'), axis=0)]
    psum x1 -> x0, waiting for transfers between devices: 155 us -> none  [body(): grad_second = lax.psum(grad_second, 'ids')]
    reduce_sum x0 -> x1, other arithmetic: none -> 15.1 us  [body(): grad_second = jnp.sum(lax.all_gather(grad_second, 'ids'), axis=0)]
  transfers between devices with their start and end apart: 12 -> 12, of which waited for: 7 -> 7; matrix products, arithmetic and copies ran while one was open for 12% -> 8% of each run, Pallas kernels for 0% -> 0%
where the time goes in v1:
time: 1500 us; the launch traced here: 1490 us
  waiting for transfers between devices  956 us (64%)
  blocking collectives  262 us (17%)
  matrix products  121 us (8%)
  other arithmetic  87.3 us (6%)
  local copies, waits for them, and re-layouts  37.5 us (2%)
  between operations  15.7 us (1%)
  starting transfers between devices  15 us (1%)
    all_gather x1, waiting for transfers between devices, body(): grad_second = jnp.sum(lax.all_gather(grad_second, 'ids'), axis=0)  634 us
    reduce_scatter x1, waiting for transfers between devices, body(): lax.psum_scatter(local_second, 'mdl', scatter_dimension=0, tiled=False)  127 us
    psum x1, waiting for transfers between devices, body(): lax.psum((jnp.stack([jnp.sum(incoming_one * unit_one, 0), jnp.sum(incomin...  110 us
    all_gather x1, blocking collectives, body(): lax.all_gather(jnp.pad(norm_params, ((0, 0), (0, more))), 'mdl', axis=1,...  48.9 us
    reduce_scatter x1, waiting for transfers between devices, body(): lax.psum_scatter(local_first, 'mdl', scatter_dimension=0, tiled=False)  47.1 us
    dot_general x11, matrix products, contract(): lax.dot_general(left, right, (((left_dim,), (right_dim,)), ((), ())), pre...  45.5 us
    psum x1, blocking collectives, body(): lax.psum((jnp.stack([jnp.sum(incoming_one * unit_one, 0), jnp.sum(incomin...  40.7 us
    psum x1, blocking collectives, body(): lax.psum(jnp.stack([jnp.sum(incoming_two * unit_two, 0), jnp.sum(incoming...  40.2 us
  transfers between devices with their start and end apart: 12, of which 7 were waited for; matrix products, arithmetic and copies ran while one was open for 8% of the time, Pallas kernels for 0%

profile of v1, /device:TPU:0, one launch (start us, length us, event | category | flops | bytes accessed | tf_op | source)
XLA Modules:
  0.0 1494.5 jit_solution(9010512587461533780)
XLA Ops:
  9.8 13.0 subtract_convert_fusion
  26.4 18.5 %all_to_all.48 = bf16[8,2,8192]{2,1,0:T(2,128)(2,1)S(1)} all-to-all(bf16[8,2,8192]{2,1,0:T(2,128)(2,1)S(1)} %reshape.106), channel_id=1, replica_groups=mesh['ids'=8,'mdl'=4] {'ids'}, dimensions={0} | all-to-all | bytes 524288 | tf_op jit(solution)/shard_map/all_to_all | solution.py:141
  81.7 48.9 %all_gather.30 = f32[4,2048]{1,0:T(4,128)S(1)} all-gather(f32[4,512]{1,0:T(4,128)S(1)} %pad.17), channel_id=1, replica_groups=mesh['ids'=8,'mdl'=4] {'mdl'}, dimensions={1}, use_global_device_ids=true | all-gather | bytes 40960 | tf_op jit(solution)/shard_map/all_gather | solution.py:118
  147.0 11.5 multiply_reduce_fusion.1
  158.5 39.1 %all-reduce.6 = (f32[2,2048]{1,0:T(2,128)S(1)}, f32[]{:T(128)}) all-reduce(f32[2,2048]{1,0:T(2,128)S(1)} %pad_maximum_fusion.3, f32[]{:T(128)} %get-tuple-element.151), channel_id=1, replica_groups=mesh['ids'=8,'mdl'=4] {'ids','mdl'}, use_global_device_ids=true, to_apply=%region_2.3 | all-reduce | flops 4097 | bytes 32776 | tf_op jit(solution)/shard_map/psum | solution.py:160
  198.9 7.3 add_convert_fusion.1
  206.2 18.3 %multiply_reduce_fusion = (f32[2048]{0:T(1024)S(1)}, f32[2048]{0:T(1024)S(1)}, f32[1024,2048]{1,0:T(8,128)}, f32[1024,2048]{1,0:T(8,128)}) fusion(f32[1024]{0:T(1024)S(1)} %bitcast.110, bf16[1024,2048]{1,0:T(8,128)(2,1)} %add_convert_fusion.1, bf16[2048,2048]{0,1:T(8,128)(2,1)} %all-gather.12.cloned.1.call-done), kind=kOutput, calls=%fused_computation.17 | convolution fusion | flops 8612999168 | bytes 29380608 | tf_op jit(solution)/shard_map/dot_general | solution.py:165
  224.5 40.1 %psum.51 = f32[2,2048]{1,0:T(2,128)S(1)} all-reduce(f32[2,2048]{1,0:T(2,128)S(1)} %pad_maximum_fusion.4), channel_id=1, replica_groups=mesh['ids'=8,'mdl'=4] {'ids','mdl'}, use_global_device_ids=true, to_apply=%region_7.8 | all-reduce | flops 4096 | bytes 32768 | tf_op jit(solution)/shard_map/psum | solution.py:168
  274.9 40.2 %psum.52 = f32[2,2048]{1,0:T(2,128)S(1)} all-reduce(f32[2,2048]{1,0:T(2,128)S(1)} %pad_maximum_fusion.5), channel_id=1, replica_groups=mesh['ids'=8,'mdl'=4] {'ids','mdl'}, use_global_device_ids=true, to_apply=%region_10.11 | all-reduce | flops 4096 | bytes 32768 | tf_op jit(solution)/shard_map/psum | solution.py:198
  315.1 12.7 multiply_convert_fusion.1
  327.8 18.4 %multiply_reduce_fusion.2 = (f32[2048]{0:T(1024)S(1)}, f32[2048]{0:T(1024)S(1)}, f32[1024,2048]{1,0:T(8,128)}) fusion(f32[2048]{0:T(1024)S(1)} %bitcast.94, f32[2048]{0:T(1024)S(1)} %bitcast.97, f32[1024,2048]{1,0:T(8,128)} %get-tuple-element.164, bf16[1024,2048]{1,0:T(8,128)(2,1)S(1)} %multiply_convert_fusion.1, ...), kind=kOutput, calls=%fused_computation.24 | convolution fusion | flops 8615096320 | bytes 29392896 | tf_op jit(solution)/shard_map/dot_general | solution.py:36
  346.2 40.7 %all-reduce.5 = (f32[2,2048]{1,0:T(2,128)S(1)}, f32[32]{0:T(128)S(1)}) all-reduce(f32[2,2048]{1,0:T(2,128)S(1)} %pad_maximum_fusion.6, f32[32]{0:T(128)S(1)} %get-tuple-element.144), channel_id=1, replica_groups=mesh['ids'=8,'mdl'=4] {'ids','mdl'}, use_global_device_ids=true, to_apply=%region_13.14 | all-reduce | flops 4128 | bytes 33024 | tf_op jit(solution)/shard_map/psum | solution.py:224
  386.9 11.3 multiply_convert_fusion
  431.8 47.1 %reduce-scatter.4.cloned.1.call-done = f32[1,1024,512]{2,1,0:T(8,128)} async-done(((f32[4,1024,512]{2,1,0:T(8,128)}), f32[1,1024,512]{2,1,0:T(8,128)}) %reduce-scatter.4.cloned.1.call-update) | async-done | bytes 2097168 | tf_op jit(solution)/shard_map/reduce_scatter | solution.py:249
  479.0 127.4 %reduce-scatter.8.cloned.1.call-done = f32[1,2048,512]{2,1,0:T(8,128)} async-done(((f32[4,2048,512]{2,1,0:T(8,128)}), f32[1,2048,512]{2,1,0:T(8,128)}) %reduce-scatter.8.cloned.1.call-update) | async-done | bytes 4194320 | tf_op jit(solution)/shard_map/reduce_scatter | solution.py:220
  613.7 6.8 fusion.18
  630.0 109.6 %all-reduce.9.cloned.1.call-done = f32[2048,32]{0,1:T(8,128)} async-done(((f32[2048,32]{0,1:T(8,128)}), f32[2048,32]{0,1:T(8,128)}) %all-reduce.9.cloned.1.call-update) | async-done | bytes 262160 | tf_op jit(solution)/shard_map/psum | solution.py:224
  742.6 15.7 %all_gather.37 = bf16[8,1024,32]{2,1,0:T(8,128)(2,1)S(1)} all-gather(bf16[8,256,32]{2,1,0:T(8,128)(2,1)S(1)} %reshape.98), channel_id=1, replica_groups=mesh['ids'=8,'mdl'=4] {'mdl'}, dimensions={1}, use_global_device_ids=true | all-gather | bytes 655360 | tf_op jit(solution)/shard_map/all_gather | solution.py:185
  758.3 14.1 fusion.19
  772.4 7.5 all_gather.38
  779.9 30.7 %reduce-scatter.6.cloned.1.call-done = f32[128,512]{1,0:T(8,128)} async-done(((f32[1024,512]{1,0:T(8,128)}), f32[128,512]{1,0:T(8,128)}) %reduce-scatter.6.cloned.1.call-update) | async-done | bytes 262160 | tf_op jit(solution)/shard_map/reduce_scatter | solution.py:250
  815.0 633.9 %all-gather.14.cloned.1.call-done = f32[8,2048,512]{2,1,0:T(8,128)} async-done(((f32[1,2048,512]{2,1,0:T(8,128)}), f32[8,2048,512]{2,1,0:T(8,128)}) %all-gather.14.cloned.1.call-update) | async-done | bytes 33554448 | tf_op jit(solution)/shard_map/all_gather | solution.py:221
  1448.9 15.1 %reduce_sum.108 = f32[2048,512]{1,0:T(8,128)} reduce(f32[8,2048,512]{2,1,0:T(8,128)} %all-gather.14.cloned.1.call-done, f32[]{:T(128)} %constant.41.clone.1), dimensions={0}, to_apply=%region_17.18 | reduce | flops 7340032 | bytes 37748740 | tf_op jit(solution)/shard_map/reduce_sum | solution.py:221
  1477.8 9.0 fusion.48
  (157 shorter events, 142.0 us)
Async XLA Ops:
  7.2 46.1 %all-gather.6.cloned.1.call-start = ((), (), s32[]{:S(2)}) async-start(), calls=%async_computation.7 | async-start | bytes 1179648 | tf_op jit(solution)/shard_map/all_gather | solution.py:109
  9.0 129.6 %all-gather.10.cloned.1.call-start = ((), (), s32[]{:S(2)}) async-start(), calls=%async_computation.9 | async-start | bytes 1310720 | tf_op jit(solution)/shard_map/all_gather | solution.py:142
  48.2 98.8 %all-gather.8.cloned.1.call-start = ((), (), s32[]{:S(2)}) async-start(), calls=%async_computation.8 | async-start | bytes 5242880 | tf_op jit(solution)/shard_map/all_gather | solution.py:110
  53.3 152.9 %all-gather.12.cloned.1.call-start = ((), (), s32[]{:S(2)}) async-start(), calls=%async_computation.10 | async-start | bytes 10485760 | tf_op jit(solution)/shard_map/all_gather | solution.py:115
  66.3 11.7 all-to-all-start
  78.0 68.4 %copy-start.12 = (s32[8,1,1024]{2,1,0:T(1,128)}, s32[8,1,1024]{2,1,0:T(1,128)S(1)}, u32[]{:S(2)}) copy-start(s32[8,1,1024]{2,1,0:T(1,128)S(1)} %all-to-all-done) | copy-start | bytes 98308
  78.0 58.2 %all-to-all-start.1 = ((bf16[4,1024,256]{2,1,0:T(8,128)(2,1)}), bf16[4,1024,256]{2,1,0:T(8,128)(2,1)S(1)}, u32[]{:S(2)}, u32[]{:S(2)}) async-start(bf16[4,1024,256]{2,1,0:T(8,128)(2,1)} %bitcast.3), calls=%async_computation.1 | async-start | bytes 4194304 | tf_op jit(solution)/shard_map/all_to_all | solution.py:120
  81.6 397.3 %reduce-scatter.4.cloned.1.call-start = ((), (), s32[]{:S(2)}) async-start(), calls=%async_computation.11 | async-start | bytes 10485760 | tf_op jit(solution)/shard_map/reduce_scatter | solution.py:249
  206.2 59.3 %copy-start.21 = (f32[32]{0:T(128)S(1)}, f32[32]{0:T(128)}, u32[]{:S(2)}) copy-start(f32[32]{0:T(128)} %param.29) | copy-start | bytes 388
  406.9 199.5 %reduce-scatter.8.cloned.1.call-start = ((), (), s32[]{:S(2)}) async-start(), calls=%async_computation.13 | async-start | bytes 20971520 | tf_op jit(solution)/shard_map/reduce_scatter | solution.py:220
  426.0 180.5 %copy-start.7 = (f32[128,450]{0,1:T(8,128)S(1)}, f32[128,450]{0,1:T(8,128)}, u32[]{:S(2)}) copy-start(f32[128,450]{0,1:T(8,128)} %param.25) | copy-start | bytes 691204
  426.0 180.7 %copy-start.10 = (f32[128,450]{0,1:T(8,128)S(1)}, f32[128,450]{0,1:T(8,128)}, u32[]{:S(2)}) copy-start(f32[128,450]{0,1:T(8,128)} %param.31) | copy-start | bytes 691204
  426.0 180.8 %copy-start.11 = (f32[128,450]{0,1:T(8,128)S(1)}, f32[128,450]{0,1:T(8,128)}, u32[]{:S(2)}) copy-start(f32[128,450]{0,1:T(8,128)} %param.30) | copy-start | bytes 691204
  426.0 313.6 %all-reduce.9.cloned.1.call-start = ((), (), s32[]{:S(2)}) async-start(), calls=%async_computation.15 | async-start | bytes 524288 | tf_op jit(solution)/shard_map/psum | solution.py:224
  431.8 378.8 %reduce-scatter.6.cloned.1.call-start = ((), (), s32[]{:S(2)}) async-start(), calls=%async_computation.12 | async-start | bytes 2359296 | tf_op jit(solution)/shard_map/reduce_scatter | solution.py:250
  478.9 970.0 %all-gather.14.cloned.1.call-start = ((), (), s32[]{:S(2)}) async-start(), calls=%async_computation.14 | async-start | bytes 37748736 | tf_op jit(solution)/shard_map/all_gather | solution.py:221
  606.6 22.7 %copy-start.16 = (f32[4,450]{1,0:T(4,128)S(1)}, f32[4,450]{1,0:T(4,128)}, u32[]{:S(2)}) copy-start(f32[4,450]{1,0:T(4,128)} %param.28) | copy-start | bytes 21604
  606.6 22.7 %copy-start.18 = (f32[4,450]{1,0:T(4,128)S(1)}, f32[4,450]{1,0:T(4,128)}, u32[]{:S(2)}) copy-start(f32[4,450]{1,0:T(4,128)} %param.37) | copy-start | bytes 21604
  606.6 22.7 %copy-start.19 = (f32[4,450]{1,0:T(4,128)S(1)}, f32[4,450]{1,0:T(4,128)}, u32[]{:S(2)}) copy-start(f32[4,450]{1,0:T(4,128)} %param.36) | copy-start | bytes 21604
  606.7 133.0 %copy-start.9 = (f32[450,32]{0,1:T(8,128)S(1)}, f32[450,32]{0,1:T(8,128)}, u32[]{:S(2)}) copy-start(f32[450,32]{0,1:T(8,128)} %param.27) | copy-start | bytes 172804
  606.7 133.0 %copy-start.13 = (f32[450,32]{0,1:T(8,128)S(1)}, f32[450,32]{0,1:T(8,128)}, u32[]{:S(2)}) copy-start(f32[450,32]{0,1:T(8,128)} %param.35) | copy-start | bytes 172804
  606.7 133.0 %copy-start.14 = (f32[450,32]{0,1:T(8,128)S(1)}, f32[450,32]{0,1:T(8,128)}, u32[]{:S(2)}) copy-start(f32[450,32]{0,1:T(8,128)} %param.34) | copy-start | bytes 172804
  613.7 144.6 %dynamic-slice-start = ((s32[8192]{0:T(1024)}, s32[]{:T(128)}), s32[2048]{0:T(1024)S(1)}, s32[]{:S(2)}) async-start(s32[8192]{0:T(1024)} %param.23, s32[]{:T(128)} %select_n.30), calls=%async_computation.16 | async-start | bytes 16896 | tf_op jit(solution)/shard_map/dynamic_slice | solution.py:187
  623.3 118.1 %all-to-all-start.3 = ((bf16[8,2,4096]{2,1,0:T(2,128)(2,1)}), bf16[8,2,4096]{2,1,0:T(2,128)(2,1)S(1)}, u32[]{:S(2)}, u32[]{:S(2)}) async-start(bf16[8,2,4096]{2,1,0:T(2,128)(2,1)} %reshape.108), calls=%async_computation.3 | async-start | bytes 262144 | tf_op jit(solution)/shard_map/all_to_all | solution.py:184
  (13 other events, 164.2 us)
Sparse Core Ops, SparseCore 0:
  10.6 42.5 all-gather.5
  55.4 17.2 all-gather.9
  74.3 56.9 all-gather.7
  133.3 57.1 all-gather.11
  407.0 71.8 reduce-scatter.3
  481.3 125.0 reduce-scatter.7
  612.5 127.0 all-reduce.8
  743.2 67.4 reduce-scatter.5
  812.2 636.6 all-gather.13
